TPU v7x, 32 devices: a whole 2x2x4 slice. The times are simulated.
32 devices in a mesh: tile: 8 (over y, x, core), sect: 2 (over z_hi), lev: 2 (over z_lo).
Axes of the slice: x: 2, y: 2, z: 4 (z_hi: 2, z_lo: 2; z = z_hi * 2 + z_lo), core: 2. Of those that a mesh axis runs over, the one named last changes fastest.
Arguments:
- adjoint: float32 [2, 8, 64, 128, 128], P('sect', 'tile', 'lev'), may hold values from -6 to 6
- diffusion: float32 [2, 8, 128, 128], P('sect', 'tile'), may hold values from 0.02 to 0.12
- wet_mask: int32 [2, 8, 128, 128], P('sect', 'tile'), may hold values 0 or 1
- remap: int32 [2, 8, 128], P('sect', 'tile'), may hold values from 0 to 127
- coupling: float32 [2, 64], P('sect', 'lev'), may hold values from 0.1 to 0.5
- vert_inverse: float32 [2, 8, 64, 64], P('sect', 'tile')
- nbr_tile: int32 [8, 4], P('tile'), may hold values from -1 to 7, as said below
- nbr_side: int32 [8, 4], P('tile'), may hold values from 0 to 3
- nbr_flip: int32 [8, 4], P('tile'), may hold values from 0 to 1
Outputs:
- result: float32 [2, 8, 64, 128, 128], P('sect', 'tile', 'lev')
Inputs may be any that keep to these rules, and one draw needn't show every extreme that they name: `nbr_tile`: A side with a neighbour is named back by that neighbour's named side with the same flip.
All inputs are finite; a program needn't handle non-finite values. No bound on the sum of `wet_mask` on one device may be relied on, other than what follows from the above.
Results may differ from a plain program's by a relative error of at most 0.0001.
Values sent between devices are 32-bit elements; how exact they have to be, the bound alone decides.
No kernel may reach another device: no remote copies, remote signals or barrier semaphores. Data moves between devices by JAX's collectives and lax.ppermute only.
A program may use at most 64 MiB of HBM per device.

v0:
```python
import jax
import jax.numpy as jnp
from jax import lax
from jax.sharding import PartitionSpec as P


def swapped(block, axis, bit):
    count = lax.axis_size(axis)
    route = []
    for low in range(count):
        high = low | 1 << bit
        if high != low and high < count:
            route += [(low, high), (high, low)]
    return lax.ppermute(block, axis, route)


def edge_rows(field):
    return jnp.stack(
        [field[..., 0, :], field[..., -1, :], field[..., :, 0], field[..., :, -1]], axis=-3
    )


def oriented(picked, flips):
    return jnp.where((flips == 1)[:, :, None, None], picked[..., ::-1], picked)


def laplace(field, halo):
    side_cells = field.shape[3]
    position = lax.broadcasted_iota(jnp.int32, (1, 1, 1, side_cells), 3)
    upper = jnp.concatenate([halo[:, 0][:, :, None, :], field[:, :, :-1, :]], axis=2)
    lower = jnp.concatenate([field[:, :, 1:, :], halo[:, 1][:, :, None, :]], axis=2)
    left_side = jnp.pad(field[:, :, :, :-1], ((0, 0), (0, 0), (0, 0), (1, 0)))
    left_side = left_side + jnp.where(position == 0, halo[:, 2][:, :, :, None], jnp.float32(0.0))
    right_side = jnp.pad(field[:, :, :, 1:], ((0, 0), (0, 0), (0, 0), (0, 1)))
    right_side = right_side + jnp.where(
        position == side_cells - 1, halo[:, 3][:, :, :, None], jnp.float32(0.0)
    )
    return upper + lower + left_side + right_side - 4.0 * field


def pick_tile_rows(field, rows):
    return field[:, rows, :]


def on_device(
    adjoint, diffusion, wet_mask, remap, coupling, vert_inverse, nbr_tile, nbr_side, nbr_flip
):
    current = adjoint[0]
    diffusivity = diffusion[0]
    wet_cells = wet_mask[0].astype(jnp.float32)
    remap_rows = remap[0]
    level_gain = coupling[0]
    inverse = vert_inverse[0]
    level_rows = current.shape[1]
    my_first = lax.axis_index("lev") * level_rows
    for step in range(2):
        partner = swapped(current, "sect", 0)
        pulled = jax.vmap(pick_tile_rows)(partner, remap_rows)
        coupled = current + level_gain[None, :, None, None] * pulled
        whole = lax.all_gather(coupled, "lev", axis=1, tiled=True)
        own_columns = lax.dynamic_slice_in_dim(inverse, my_first, level_rows, 2)
        column = jnp.einsum("tkl,tkxy->tlxy", own_columns, whole, precision=lax.Precision.HIGHEST)
        flux = wet_cells[:, None] * diffusivity[:, None] * column
        edges = edge_rows(flux)
        all_edges = lax.all_gather(edges, "tile", axis=0, tiled=True)
        picked = all_edges[jnp.maximum(nbr_tile, 0), nbr_side]
        halo = jnp.where(
            (nbr_tile >= 0)[:, :, None, None], oriented(picked, nbr_flip), jnp.float32(0.0)
        )
        current = wet_cells[:, None] * (column + laplace(flux, halo))
    return current[None]


def solution(mesh):
    in_specs = (
        P("sect", "tile", "lev", None, None),
        P("sect", "tile", None, None),
        P("sect", "tile", None, None),
        P("sect", "tile", None),
        P("sect", "lev"),
        P("sect", "tile", None, None),
        P("tile", None),
        P("tile", None),
        P("tile", None),
    )
    out_specs = P("sect", "tile", "lev", None, None)
    return jax.shard_map(
        on_device, mesh=mesh, in_specs=in_specs, out_specs=out_specs, check_vma=False
    )
```

profile of v0, /device:TPU:0, one launch (start us, length us, event | category | flops | bytes accessed | tf_op | source)
XLA Modules:
  0.0 405.9 jit_solution(2878523833001333384)
XLA Ops:
  6.5 2.8 copy.65
  9.4 4.1 %collective-permute-start = (f32[1,32,128,128]{3,1,2,0:T(8,128)S(1)}, f32[1,32,128,128]{3,1,2,0:T(8,128)}, u32[]{:S(2)}, u32[]{:S(2)}) collective-permute-start(f32[1,32,128,128]{3,1,2,0:T(8,128)S(1)} %bitcast.109), channel_id=1, source_target_pairs={{0,2},{2,0},{1,3},{3,1},{4,6},{6,4},{5,7},{7,5},{8,10},{10,8},{9,1... | collective-permute-start | bytes 6291464 | tf_op jit(solution)/shard_map/ppermute | solution.py:14
  13.5 90.6 %collective-permute-done = f32[1,32,128,128]{3,1,2,0:T(8,128)} collective-permute-done((f32[1,32,128,128]{3,1,2,0:T(8,128)S(1)}, f32[1,32,128,128]{3,1,2,0:T(8,128)}, u32[]{:S(2)}, u32[]{:S(2)}) %collective-permute-start) | collective-permute-done | bytes 2097184 | tf_op jit(solution)/shard_map/ppermute | solution.py:14
  104.1 3.6 gather_fusion.2
  107.8 4.2 %fusion.16 = f32[1,32,128,128]{3,1,2,0:T(8,128)} fusion(f32[128,32,128]{2,1,0:T(8,128)} %gather_fusion.2, f32[32]{0:T(128)S(1)} %bitcast.114, f32[1,1,32,128,128]{4,3,2,1,0:T(8,128)S(1)} %copy-done.3), kind=kLoop, calls=%fused_computation.24 | loop fusion | flops 1048576 | bytes 6291584 | tf_op jit(solution)/shard_map/add | solution.py:59
  112.1 0.5 copy-done.7
  112.9 57.2 %all-gather.3.cloned.1.call-done = f32[1,64,128,128]{3,1,2,0:T(8,128)} async-done(((f32[1,32,128,128]{3,1,2,0:T(8,128)}), f32[1,64,128,128]{3,1,2,0:T(8,128)}) %all-gather.3.cloned.1.call-update) | async-done | bytes 4194320 | tf_op jit(solution)/shard_map/all_gather | solution.py:60
  170.1 4.0 fusion.2
  174.5 2.7 fusion.30
  177.2 2.8 fusion.31
  180.0 2.7 fusion.29
  182.7 2.7 copy.54
  185.3 2.7 copy.53
  188.0 10.0 %all_gather.13 = f32[8,4,32,128]{3,2,1,0:T(8,128)S(1)} all-gather(f32[1,4,32,128]{3,2,1,0:T(8,128)S(1)} %pad_maximum_fusion), channel_id=1, replica_groups=mesh['tile'=8,'sect'=2,'lev'=2] {'tile'}, dimensions={0}, use_global_device_ids=true | all-gather | bytes 589824 | tf_op jit(solution)/shard_map/all_gather | solution.py:65
  198.0 0.6 gather_fusion
  199.0 5.3 %fusion.8 = f32[1,32,128,128]{3,1,2,0:T(8,128)S(1)} fusion(f32[1,32,127,128]{3,1,2,0:T(8,128)} %get-tuple-element.16, f32[1,32,1,128]{3,1,2,0:T(8,128)S(1)} %get-tuple-element.28, f32[1,32,1,128]{3,1,2,0:T(8,128)S(1)} %get-tuple-element.27, f32[1,32,127,128]{3,1,2,0:T(8,128)} %get-tuple-element.15, f32[32,128,128]{2,0,1:T(8,128)S(1)} %fusion.2, ...), kind=kLoop, calls=%fused_computation.13 | loop fusion | flops 7340032 | bytes 12714240 | tf_op jit(solution)/shard_map/mul | solution.py:70
  204.3 1.3 copy-done.1
  205.6 2.4 collective-permute-start.1
  208.0 91.4 %collective-permute-done.1 = f32[1,32,128,128]{3,1,2,0:T(8,128)} collective-permute-done((f32[1,32,128,128]{3,1,2,0:T(8,128)S(1)}, f32[1,32,128,128]{3,1,2,0:T(8,128)}, u32[]{:S(2)}, u32[]{:S(2)}) %collective-permute-start.1) | collective-permute-done | bytes 2097184 | tf_op jit(solution)/shard_map/ppermute | solution.py:14
  299.4 3.6 gather_fusion.3
  303.0 3.5 fusion.15
  306.5 56.0 %all-gather.5.cloned.1.call-done = f32[1,64,128,128]{3,1,2,0:T(8,128)} async-done(((f32[1,32,128,128]{3,1,2,0:T(8,128)}), f32[1,64,128,128]{3,1,2,0:T(8,128)}) %all-gather.5.cloned.1.call-update) | async-done | bytes 4194320 | tf_op jit(solution)/shard_map/all_gather | solution.py:60
  362.5 4.0 fusion
  366.9 2.7 fusion.27
  369.6 2.8 fusion.28
  372.3 2.7 fusion.26
  375.1 2.7 copy.58
  377.7 2.7 copy.57
  380.4 9.8 %all_gather.15 = f32[8,4,32,128]{3,2,1,0:T(8,128)S(1)} all-gather(f32[1,4,32,128]{3,2,1,0:T(8,128)S(1)} %pad_maximum_fusion.1), channel_id=1, replica_groups=mesh['tile'=8,'sect'=2,'lev'=2] {'tile'}, dimensions={0}, use_global_device_ids=true | all-gather | bytes 589824 | tf_op jit(solution)/shard_map/all_gather | solution.py:65
  390.2 0.6 gather_fusion.1
  391.1 5.3 %fusion.14 = f32[1,1,32,128,128]{4,2,3,1,0:T(8,128)S(1)} fusion(f32[1,32,127,128]{3,1,2,0:T(8,128)} %get-tuple-element.8, f32[1,32,1,128]{3,1,2,0:T(8,128)S(1)} %get-tuple-element.24, f32[1,32,1,128]{3,1,2,0:T(8,128)S(1)} %get-tuple-element.23, f32[1,32,127,128]{3,1,2,0:T(8,128)} %get-tuple-element.7, f32[32,128,128]{2,0,1:T(8,128)S(1)} %fusion, ...), kind=kLoop, calls=%fused_computation.20 | loop fusion | flops 7340032 | bytes 12714240 | tf_op jit(solution)/shard_map/broadcast_in_dim | solution.py:71
  396.5 2.5 copy.61
  (50 shorter events, 1.8 us)
Async XLA Ops:
  6.5 163.6 %copy-start = (f32[1,1,64,64]{3,2,1,0:T(8,128)S(1)}, f32[1,1,64,64]{3,2,1,0:T(8,128)}, u32[]{:S(2)}) copy-start(f32[1,1,64,64]{3,2,1,0:T(8,128)} %param.14) | copy-start | bytes 49156
  6.5 6.9 %copy-start.10 = (s32[1,1,128]{2,1,0:T(1,128)S(1)}, s32[1,1,128]{2,1,0:T(1,128)}, u32[]{:S(2)}) copy-start(s32[1,1,128]{2,1,0:T(1,128)} %param.12) | copy-start | bytes 1540
  6.5 163.6 %all-gather.3.cloned.1.call-start = ((), (), s32[]{:S(2)}) async-start(), calls=%async_computation | async-start | bytes 6291456 | tf_op jit(solution)/shard_map/all_gather | solution.py:60
  9.4 94.8 %collective-permute-start = (f32[1,32,128,128]{3,1,2,0:T(8,128)S(1)}, f32[1,32,128,128]{3,1,2,0:T(8,128)}, u32[]{:S(2)}, u32[]{:S(2)}) collective-permute-start(f32[1,32,128,128]{3,1,2,0:T(8,128)S(1)} %bitcast.109), channel_id=1, source_target_pairs={{0,2},{2,0},{1,3},{3,1},{4,6},{6,4},{5,7},{7,5},{8,10},{10,8},{9,1... | collective-permute-start | bytes 6291464 | tf_op jit(solution)/shard_map/ppermute | solution.py:14
  13.5 94.2 %copy-start.3 = (f32[1,1,32,128,128]{4,3,2,1,0:T(8,128)S(1)}, f32[1,1,32,128,128]{4,3,2,1,0:T(8,128)}, u32[]{:S(2)}) copy-start(f32[1,1,32,128,128]{4,3,2,1,0:T(8,128)} %param.9) | copy-start | bytes 6291460
  13.5 94.2 %copy-start.6 = (f32[1,32]{1,0:T(1,128)S(1)}, f32[1,32]{1,0:T(1,128)}, u32[]{:S(2)}) copy-start(f32[1,32]{1,0:T(1,128)} %param.13) | copy-start | bytes 388
  112.0 0.7 copy-start.7
  112.0 0.7 copy-start.8
  112.0 0.7 copy-start.9
  112.0 0.9 copy-start.4
  112.0 0.9 copy-start.5
  112.0 250.5 %all-gather.5.cloned.1.call-start = ((), (), s32[]{:S(2)}) async-start(), calls=%async_computation.1 | async-start | bytes 6291456 | tf_op jit(solution)/shard_map/all_gather | solution.py:60
  204.3 1.3 copy-start.1
  205.6 93.8 %collective-permute-start.1 = (f32[1,32,128,128]{3,1,2,0:T(8,128)S(1)}, f32[1,32,128,128]{3,1,2,0:T(8,128)}, u32[]{:S(2)}, u32[]{:S(2)}) collective-permute-start(f32[1,32,128,128]{3,1,2,0:T(8,128)S(1)} %fusion.8), channel_id=1, source_target_pairs={{0,2},{2,0},{1,3},{3,1},{4,6},{6,4},{5,7},{7,5},{8,10},{10,8},{9,1... | collective-permute-start | bytes 6291464 | tf_op jit(solution)/shard_map/ppermute | solution.py:14
  208.0 95.0 %copy-start.2 = (f32[1,32,128,128]{3,1,2,0:T(8,128)S(1)}, f32[1,32,128,128]{3,1,2,0:T(8,128)}, u32[]{:S(2)}) copy-start(f32[1,32,128,128]{3,1,2,0:T(8,128)} %copy-done.1) | copy-start | bytes 6291460
Sparse Core Ops, SparseCore 0:
  112.2 57.9 all-gather.2
  306.6 55.8 all-gather.4
where the time goes:
time: 406 us
  waiting for transfers between devices  295 us (73%)
  local copies, waits for them, and re-layouts  43.3 us (11%)
  blocking collectives  19.8 us (5%)
  other arithmetic  19.3 us (5%)
  between operations  13.6 us (3%)
  matrix products  8 us (2%)
  starting transfers between devices  6.55 us (2%)
    ppermute x2, waiting for transfers between devices, swapped(): return lax.ppermute(block, axis, route)  182 us
    all_gather x2, waiting for transfers between devices, on_device(): whole = lax.all_gather(coupled, 'lev', axis=1, tiled=True)  113 us
    all_gather x2, blocking collectives, on_device(): all_edges = lax.all_gather(edges, 'tile', axis=0, tiled=True)  19.8 us
    slice x4, local copies, waits for them, and re-layouts, edge_rows(): field[..., :, 0]  10.8 us
  transfers between devices with their start and end apart: 4, of which 4 were waited for; matrix products, arithmetic and copies ran while one was open for 0% of the time, Pallas kernels for 0%

commit v1 on v0

--- a/solution.py
+++ b/solution.py
@@ -62,7 +62,15 @@
         column = jnp.einsum("tkl,tkxy->tlxy", own_columns, whole, precision=lax.Precision.HIGHEST)
         flux = wet_cells[:, None] * diffusivity[:, None] * column
         edges = edge_rows(flux)
-        all_edges = lax.all_gather(edges, "tile", axis=0, tiled=True)
+        ways, here, step_2 = (lax.axis_size("tile"), lax.axis_index("tile"), edges.shape[0])
+        line, have = (edges, 1)
+        while have < ways:
+            line = jnp.concatenate(
+                [line, lax.ppermute(line, "tile", [(d, (d - have) % ways) for d in range(ways)])],
+                axis=0,
+            )
+            have = 2 * have
+        all_edges = jnp.roll(line, here * step_2, axis=0)
         picked = all_edges[jnp.maximum(nbr_tile, 0), nbr_side]
         halo = jnp.where(
             (nbr_tile >= 0)[:, :, None, None], oriented(picked, nbr_flip), jnp.float32(0.0)

time: 406 us -> 414 us (1.020)
  blocking collectives: 19.8 us -> 0 us
  waiting for transfers between devices: 295 us -> 313 us
  starting transfers between devices: 6.55 us -> 13.5 us
    all_gather x2 -> x0, blocking collectives: 19.8 us -> none  [on_device(): all_edges = lax.all_gather(edges, 'tile', axis=0, tiled=True)]
    ppermute x0 -> x6, waiting for transfers between devices: none -> 17.8 us  [on_device(): lax.ppermute(line, 'tile', [(d, (d - have) % ways) for d in range(ways)])]
    ppermute x0 -> x6, starting transfers between devices: none -> 6.87 us  [on_device(): lax.ppermute(line, 'tile', [(d, (d - have) % ways) for d in range(ways)])]
    slice x2 -> x4, local copies, waits for them, and re-layouts: 5.31 us -> 10.8 us  [edge_rows(): field[..., :, -1]]
    slice x4 -> x2, local copies, waits for them, and re-layouts: 10.8 us -> 5.31 us  [edge_rows(): field[..., :, 0]]
  transfers between devices with their start and end apart: 4 -> 10, of which waited for: 4 -> 10; matrix products, arithmetic and copies ran while one was open for 0% -> 3% of each run, Pallas kernels for 0% -> 0%
where the time goes in v1:
time: 414 us; the launch traced here: 413 us
  waiting for transfers between devices  313 us (76%)
  local copies, waits for them, and re-layouts  43.9 us (11%)
  other arithmetic  21 us (5%)
  between operations  13.6 us (3%)
  starting transfers between devices  13.5 us (3%)
  matrix products  7.99 us (2%)
    ppermute x2, waiting for transfers between devices, swapped(): return lax.ppermute(block, axis, route)  181 us
    all_gather x2, waiting for transfers between devices, on_device(): whole = lax.all_gather(coupled, 'lev', axis=1, tiled=True)  115 us
    ppermute x6, waiting for transfers between devices, on_device(): lax.ppermute(line, 'tile', [(d, (d - have) % ways) for d in range(ways)])  17.8 us
    slice x4, local copies, waits for them, and re-layouts, edge_rows(): field[..., :, -1]  10.8 us
  transfers between devices with their start and end apart: 10, of which 10 were waited for; matrix products, arithmetic and copies ran while one was open for 3% of the time, Pallas kernels for 0%

profile of v1, /device:TPU:0, one launch (start us, length us, event | category | flops | bytes accessed | tf_op | source)
XLA Modules:
  0.0 413.0 jit_solution(12528891724749206213)
XLA Ops:
  6.5 2.8 copy.54
  9.4 4.1 collective-permute-start
  13.5 90.6 %collective-permute-done = f32[1,32,128,128]{3,1,2,0:T(8,128)} collective-permute-done((f32[1,32,128,128]{3,1,2,0:T(8,128)S(1)}, f32[1,32,128,128]{3,1,2,0:T(8,128)}, u32[]{:S(2)}, u32[]{:S(2)}) %collective-permute-start) | collective-permute-done | bytes 2097184 | tf_op jit(solution)/shard_map/ppermute | solution.py:14
  104.1 3.6 gather_fusion.2
  107.8 4.2 %fusion.16 = f32[1,32,128,128]{3,1,2,0:T(8,128)} fusion(f32[128,32,128]{2,1,0:T(8,128)} %gather_fusion.2, f32[32]{0:T(128)S(1)} %bitcast.126, f32[1,1,32,128,128]{4,3,2,1,0:T(8,128)S(1)} %copy-done.3), kind=kLoop, calls=%fused_computation.24 | loop fusion | flops 1048576 | bytes 6291584 | tf_op jit(solution)/shard_map/add | solution.py:59
  112.9 57.2 %all-gather.3.cloned.1.call-done = f32[1,64,128,128]{3,1,2,0:T(8,128)} async-done(((f32[1,32,128,128]{3,1,2,0:T(8,128)}), f32[1,64,128,128]{3,1,2,0:T(8,128)}) %all-gather.3.cloned.1.call-update) | async-done | bytes 4194320 | tf_op jit(solution)/shard_map/all_gather | solution.py:60
  170.1 4.0 fusion.2
  175.5 2.8 fusion.57
  178.3 2.7 copy.42
  180.9 2.7 copy.43
  185.5 1.9 collective-permute-done.1
  188.2 2.8 fusion.55
  190.9 2.5 collective-permute-done.2
  194.3 2.6 fusion.56
  197.0 4.5 %collective-permute-done.3 = f32[4,4,32,128]{3,2,1,0:T(8,128)S(1)} collective-permute-done((f32[4,4,32,128]{3,2,1,0:T(8,128)S(1)}, f32[4,4,32,128]{3,2,1,0:T(8,128)S(1)}, u32[]{:S(2)}, u32[]{:S(2)}) %collective-permute-start.3) | collective-permute-done | bytes 262176 | tf_op jit(solution)/shard_map/ppermute | solution.py:69
  202.9 5.7 %fusion.8 = f32[1,32,128,128]{3,1,2,0:T(8,128)S(1)} fusion(f32[1,32,127,128]{3,1,2,0:T(8,128)} %get-tuple-element.17, f32[1,32,1,128]{3,1,2,0:T(8,128)S(1)} %get-tuple-element.29, f32[1,32,1,128]{3,1,2,0:T(8,128)S(1)} %get-tuple-element.28, f32[1,32,127,128]{3,1,2,0:T(8,128)} %get-tuple-element.16, f32[32,128,128]{2,0,1:T(8,128)} %copy-done.2, ...), kind=kLoop, calls=%fused_computation.13 | loop fusion | flops 7340032 | bytes 12714240 | tf_op jit(solution)/shard_map/mul | solution.py:78
  208.6 2.5 collective-permute-start.4
  211.1 89.9 %collective-permute-done.4 = f32[1,32,128,128]{3,1,2,0:T(8,128)} collective-permute-done((f32[1,32,128,128]{3,1,2,0:T(8,128)S(1)}, f32[1,32,128,128]{3,1,2,0:T(8,128)}, u32[]{:S(2)}, u32[]{:S(2)}) %collective-permute-start.4) | collective-permute-done | bytes 2097184 | tf_op jit(solution)/shard_map/ppermute | solution.py:14
  300.9 3.6 gather_fusion.3
  304.5 3.5 fusion.15
  308.0 57.4 %all-gather.5.cloned.1.call-done = f32[1,64,128,128]{3,1,2,0:T(8,128)} async-done(((f32[1,32,128,128]{3,1,2,0:T(8,128)}), f32[1,64,128,128]{3,1,2,0:T(8,128)}) %all-gather.5.cloned.1.call-update) | async-done | bytes 4194320 | tf_op jit(solution)/shard_map/all_gather | solution.py:60
  365.4 4.0 fusion
  370.8 2.8 fusion.54
  373.5 2.7 copy.46
  376.2 2.7 copy.47
  380.7 1.9 collective-permute-done.5
  383.3 2.8 fusion.52
  386.0 2.5 collective-permute-done.6
  389.4 2.6 fusion.53
  392.0 4.5 %collective-permute-done.7 = f32[4,4,32,128]{3,2,1,0:T(8,128)S(1)} collective-permute-done((f32[4,4,32,128]{3,2,1,0:T(8,128)S(1)}, f32[4,4,32,128]{3,2,1,0:T(8,128)S(1)}, u32[]{:S(2)}, u32[]{:S(2)}) %collective-permute-start.7) | collective-permute-done | bytes 262176 | tf_op jit(solution)/shard_map/ppermute | solution.py:69
  397.9 5.7 %fusion.14 = f32[1,1,32,128,128]{4,2,3,1,0:T(8,128)S(1)} fusion(f32[1,32,127,128]{3,1,2,0:T(8,128)} %get-tuple-element.9, f32[1,32,1,128]{3,1,2,0:T(8,128)S(1)} %get-tuple-element.25, f32[1,32,1,128]{3,1,2,0:T(8,128)S(1)} %get-tuple-element.24, f32[1,32,127,128]{3,1,2,0:T(8,128)} %get-tuple-element.8, f32[32,128,128]{2,0,1:T(8,128)} %copy-done.1, ...), kind=kLoop, calls=%fused_computation.20 | loop fusion | flops 7340032 | bytes 12714240 | tf_op jit(solution)/shard_map/broadcast_in_dim | solution.py:79
  403.7 2.5 copy.50
  (66 shorter events, 13.3 us)
Async XLA Ops:
  6.5 163.6 %copy-start = (f32[1,1,64,64]{3,2,1,0:T(8,128)S(1)}, f32[1,1,64,64]{3,2,1,0:T(8,128)}, u32[]{:S(2)}) copy-start(f32[1,1,64,64]{3,2,1,0:T(8,128)} %param.16) | copy-start | bytes 49156
  6.5 6.9 %copy-start.10 = (s32[1,1,128]{2,1,0:T(1,128)S(1)}, s32[1,1,128]{2,1,0:T(1,128)}, u32[]{:S(2)}) copy-start(s32[1,1,128]{2,1,0:T(1,128)} %param.14) | copy-start | bytes 1540
  6.5 163.6 %all-gather.3.cloned.1.call-start = ((), (), s32[]{:S(2)}) async-start(), calls=%async_computation | async-start | bytes 6291456 | tf_op jit(solution)/shard_map/all_gather | solution.py:60
  9.4 94.8 %collective-permute-start = (f32[1,32,128,128]{3,1,2,0:T(8,128)S(1)}, f32[1,32,128,128]{3,1,2,0:T(8,128)}, u32[]{:S(2)}, u32[]{:S(2)}) collective-permute-start(f32[1,32,128,128]{3,1,2,0:T(8,128)S(1)} %bitcast.109), channel_id=1, source_target_pairs={{0,2},{2,0},{1,3},{3,1},{4,6},{6,4},{5,7},{7,5},{8,10},{10,8},{9,1... | collective-permute-start | bytes 6291464 | tf_op jit(solution)/shard_map/ppermute | solution.py:14
  13.5 94.2 %copy-start.3 = (f32[1,1,32,128,128]{4,3,2,1,0:T(8,128)S(1)}, f32[1,1,32,128,128]{4,3,2,1,0:T(8,128)}, u32[]{:S(2)}) copy-start(f32[1,1,32,128,128]{4,3,2,1,0:T(8,128)} %param.11) | copy-start | bytes 6291460
  13.5 94.2 %copy-start.6 = (f32[1,32]{1,0:T(1,128)S(1)}, f32[1,32]{1,0:T(1,128)}, u32[]{:S(2)}) copy-start(f32[1,32]{1,0:T(1,128)} %param.15) | copy-start | bytes 388
  112.0 0.7 copy-start.7
  112.0 0.7 copy-start.8
  112.0 0.7 copy-start.9
  112.0 0.9 copy-start.4
  112.0 0.9 copy-start.5
  112.0 253.4 %all-gather.5.cloned.1.call-start = ((), (), s32[]{:S(2)}) async-start(), calls=%async_computation.1 | async-start | bytes 6291456 | tf_op jit(solution)/shard_map/all_gather | solution.py:60
  174.1 1.4 copy-start.2
  183.6 3.8 collective-permute-start.1
  187.4 6.1 %collective-permute-start.2 = (f32[2,4,32,128]{3,2,1,0:T(8,128)S(1)}, f32[2,4,32,128]{3,2,1,0:T(8,128)S(1)}, u32[]{:S(2)}, u32[]{:S(2)}) collective-permute-start(f32[2,4,32,128]{3,2,1,0:T(8,128)S(1)} %pad_maximum_fusion.2), channel_id=1, source_target_pairs={{0,24},{4,28},{8,0},{12,4},{16,8},{20,12},{24,16},{28,20},{1,25},{... | collective-permute-start | bytes 393224 | tf_op jit(solution)/shard_map/ppermute | solution.py:69
  193.5 8.0 %collective-permute-start.3 = (f32[4,4,32,128]{3,2,1,0:T(8,128)S(1)}, f32[4,4,32,128]{3,2,1,0:T(8,128)S(1)}, u32[]{:S(2)}, u32[]{:S(2)}) collective-permute-start(f32[4,4,32,128]{3,2,1,0:T(8,128)S(1)} %pad_maximum_fusion), channel_id=1, source_target_pairs={{0,16},{4,20},{8,24},{12,28},{16,0},{20,4},{24,8},{28,12},{1,17},{... | collective-permute-start | bytes 786440 | tf_op jit(solution)/shard_map/ppermute | solution.py:69
  208.6 92.4 %collective-permute-start.4 = (f32[1,32,128,128]{3,1,2,0:T(8,128)S(1)}, f32[1,32,128,128]{3,1,2,0:T(8,128)}, u32[]{:S(2)}, u32[]{:S(2)}) collective-permute-start(f32[1,32,128,128]{3,1,2,0:T(8,128)S(1)} %fusion.8), channel_id=1, source_target_pairs={{0,2},{2,0},{1,3},{3,1},{4,6},{6,4},{5,7},{7,5},{8,10},{10,8},{9,1... | collective-permute-start | bytes 6291464 | tf_op jit(solution)/shard_map/ppermute | solution.py:14
  369.4 1.4 copy-start.1
  378.8 3.8 collective-permute-start.5
  382.6 5.9 %collective-permute-start.6 = (f32[2,4,32,128]{3,2,1,0:T(8,128)S(1)}, f32[2,4,32,128]{3,2,1,0:T(8,128)S(1)}, u32[]{:S(2)}, u32[]{:S(2)}) collective-permute-start(f32[2,4,32,128]{3,2,1,0:T(8,128)S(1)} %pad_maximum_fusion.3), channel_id=1, source_target_pairs={{0,24},{4,28},{8,0},{12,4},{16,8},{20,12},{24,16},{28,20},{1,25},{... | collective-permute-start | bytes 393224 | tf_op jit(solution)/shard_map/ppermute | solution.py:69
  388.5 8.0 %collective-permute-start.7 = (f32[4,4,32,128]{3,2,1,0:T(8,128)S(1)}, f32[4,4,32,128]{3,2,1,0:T(8,128)S(1)}, u32[]{:S(2)}, u32[]{:S(2)}) collective-permute-start(f32[4,4,32,128]{3,2,1,0:T(8,128)S(1)} %pad_maximum_fusion.1), channel_id=1, source_target_pairs={{0,16},{4,20},{8,24},{12,28},{16,0},{20,4},{24,8},{28,12},{1,17},{... | collective-permute-start | bytes 786440 | tf_op jit(solution)/shard_map/ppermute | solution.py:69
Sparse Core Ops, SparseCore 0:
  112.2 57.9 all-gather.2
  308.2 57.1 all-gather.4
